TPU v7x, 512 devices: a whole 4x4x16 slice. The times are simulated.
512 devices in a mesh: req: 8 (over z_lo), section: 2 (over core), seq: 8 (over z_hi, y), tp: 4 (over x).
Axes of the slice: x: 4, y: 4, z: 16 (z_hi: 2, z_lo: 8; z = z_hi * 8 + z_lo), core: 2. Of those that a mesh axis runs over, the one named last changes fastest.
Arguments:
- hidden: bfloat16 [8192, 1536], P(('req', 'seq'), 'tp'), parts along dimension 0, may hold values from -2.5 to 2.5
- latent: float32 [8192, 64], P(('req', 'seq'), ('section', 'tp')), parts along dimension 0, may hold values from -6 to 6
- w_qkv: bfloat16 [2, 1536, 3, 1536], P('section', 'seq', None, 'tp'), may hold values from -0.15625 to 0.15625
- w_out: bfloat16 [2, 1536, 1536], P('section', 'tp'), may hold values from -0.625 to 0.625
- modulation: float32 [2, 3, 1536], P('section'), may hold values from -3 to 3
- final_mod: float32 [2, 1536], replicated, may hold values from -3 to 3
- w_final: bfloat16 [1536, 64], P(None, ('section', 'tp')), may hold values from -0.15625 to 0.15625
- stale_kv: bfloat16 [2, 2, 8192, 1536], P('section', None, ('req', 'seq'), 'tp'), parts along dimension 2, may hold values from -6 to 6
- text_kv: bfloat16 [2, 2, 1232, 1536], P('section', None, 'req', 'tp'), parts along dimension 2, as said below
- text_len: int32 [8], P('req'), parts along dimension 0, may hold values from 77 to 154
- patch_order: int32 [64, 4], P('req'), parts along dimension 0, may hold values from 0 to 3, each once within a row
- step_size: float32 [1], replicated, may hold values from -0.6 to -0.1
Outputs:
- latent_next: float32 [8192, 64], P(('req', 'seq'), ('section', 'tp')), parts along dimension 0
- new_kv: bfloat16 [2, 2, 8192, 1536], P('section', None, ('req', 'seq'), 'tp'), parts along dimension 2
There are 8 independent parts, one for each index of `req`. A program takes and returns all parts, laid end to end along the dimension named above; an argument that names none is the same for every part. Nothing has to cross between parts.
Inputs may be any that keep to these rules, and one draw needn't show every extreme that they name: Text tokens 0 to text_len - 1 are live, the rest of the 154 slots are padding. `patch_order`: each row is an ordering of the 4 patches of one index of seq. `text_kv`: keys and values of the text tokens.
All inputs are finite; a program needn't handle non-finite values.
Results may differ from a plain program's by a relative error of at most 0.015.
The roundings to bfloat16 on the way count: a program that leaves them out, or rounds other values in their place, can miss the bound.
Values may be sent and summed in bfloat16 or wider, within the bound.
A program may use at most 64 MiB of HBM per device.

v0:
```python
import jax
import jax.numpy as jnp
from jax import lax
from jax.sharding import PartitionSpec as P

HEAD = 64
MICRO = 4


def from_behind(value, axis, steps):
    count = lax.axis_size(axis)
    leading, last = (max(0, -steps), min(count, count - steps))
    return lax.ppermute(value, axis, [(source, source + steps) for source in range(leading, last)])


def layer_norm(row_block):
    row_block = row_block.astype(jnp.float32)
    center = row_block - jnp.mean(row_block, axis=-1, keepdims=True)
    spread = jnp.mean(center * center, axis=-1, keepdims=True)
    return center * lax.rsqrt(spread + 1e-06)


def modulate(row_block, shift_vec, scale_vec):
    return (layer_norm(row_block) * (1.0 + scale_vec) + shift_vec).astype(jnp.bfloat16)


def attend(queries, all_keys, all_values, text_keys, text_values, live_mask):
    factor = HEAD ** (-0.5)
    scores = (
        jnp.einsum("rhe,khe->hrk", queries, all_keys, preferred_element_type=jnp.float32) * factor
    )
    text_scores = (
        jnp.einsum("rhe,khe->hrk", queries, text_keys, preferred_element_type=jnp.float32) * factor
    )
    text_scores = jnp.where(live_mask[None, None, :], text_scores, -jnp.inf)
    peak_score = jnp.maximum(
        jnp.max(scores, axis=-1, keepdims=True), jnp.max(text_scores, axis=-1, keepdims=True)
    )
    weights = jnp.exp(scores - peak_score)
    text_weights = jnp.exp(text_scores - peak_score)
    total_mass = jnp.sum(weights, axis=-1, keepdims=True) + jnp.sum(
        text_weights, axis=-1, keepdims=True
    )
    prob_img = (weights / total_mass).astype(jnp.bfloat16)
    text_probs = (text_weights / total_mass).astype(jnp.bfloat16)
    attended = jnp.einsum("hrk,khe->rhe", prob_img, all_values, preferred_element_type=jnp.float32)
    attended = attended + jnp.einsum(
        "hrk,khe->rhe", text_probs, text_values, preferred_element_type=jnp.float32
    )
    return attended.astype(jnp.bfloat16).reshape(queries.shape[0], -1)


def take_fresh(new_kv_rows, column, is_valid, buffer, micro_ids):
    arrived = lax.all_gather(new_kv_rows[None], "seq", axis=0, tiled=True)
    hit_mask = (column[:, None] == micro_ids[None, :]) & is_valid
    return jnp.where(hit_mask[:, None, :, None, None], arrived[:, :, None], buffer)


def body(
    hidden,
    latent,
    w_qkv,
    w_out,
    modulation,
    final_mod,
    w_final,
    stale_kv,
    text_kv,
    text_len,
    patch_order,
    step_size,
):
    section_id = lax.axis_index("section")
    seq_id = lax.axis_index("seq")
    tp_id = lax.axis_index("tp")
    row_count, local_width = hidden.shape
    full_width = modulation.shape[2]
    patch_rows = row_count // MICRO
    seq_count = patch_order.shape[0]
    heads_here = local_width // HEAD
    shift_vec = modulation[0, 0]
    scale_vec = modulation[0, 1]
    gate_vec = modulation[0, 2]
    gate_here = lax.dynamic_slice_in_dim(gate_vec, tp_id * local_width, local_width)
    projection = lax.all_gather(w_qkv[0], "seq", axis=0, tiled=True).reshape(
        full_width, 3 * local_width
    )
    out_proj = w_out[0]
    text_keys = text_kv[0, 0].reshape(-1, heads_here, HEAD)
    text_values = text_kv[0, 1].reshape(-1, heads_here, HEAD)
    live_mask = jnp.arange(text_kv.shape[2], dtype=jnp.int32) < text_len[0]
    micro_ids = jnp.arange(MICRO, dtype=jnp.int32)
    seq_ids = jnp.arange(seq_count, dtype=jnp.int32)
    buffer = lax.all_gather(stale_kv, "seq", axis=0, tiled=True).reshape(
        seq_count, 2, MICRO, patch_rows, local_width
    )
    entry_blocks = hidden.reshape(MICRO, patch_rows, local_width)
    carried = jnp.zeros((patch_rows, local_width), jnp.bfloat16)
    finished = jnp.zeros((MICRO, patch_rows, local_width), jnp.bfloat16)
    for tick_index in range(MICRO + 1):
        micro_step = tick_index - section_id
        is_valid = (micro_step >= 0) & (micro_step < MICRO)
        clamped = jnp.clip(micro_step, 0, MICRO - 1)
        column = jnp.sum(jnp.where(micro_ids[None, :] == clamped, patch_order, 0), axis=1)
        my_patch = jnp.sum(jnp.where(seq_ids == seq_id, column, 0))
        picked = micro_ids == my_patch
        own_rows = lax.dynamic_index_in_dim(entry_blocks, my_patch, 0, keepdims=False)
        current = jnp.where(section_id == 0, own_rows, carried)
        full_rows = lax.all_gather(current, "tp", axis=1, tiled=True)
        normed = modulate(full_rows, shift_vec, scale_vec)
        joined = jnp.dot(normed, projection, preferred_element_type=jnp.float32).astype(
            jnp.bfloat16
        )
        queries = joined[:, :local_width].reshape(patch_rows, heads_here, HEAD)
        new_kv_rows = jnp.stack(
            [joined[:, local_width : 2 * local_width], joined[:, 2 * local_width :]]
        )
        buffer = take_fresh(new_kv_rows, column, is_valid, buffer, micro_ids)
        all_keys = buffer[:, 0].reshape(-1, heads_here, HEAD)
        all_values = buffer[:, 1].reshape(-1, heads_here, HEAD)
        attended = attend(queries, all_keys, all_values, text_keys, text_values, live_mask)
        partial_value = jnp.dot(attended, out_proj, preferred_element_type=jnp.float32)
        branch = lax.psum_scatter(partial_value, "tp", scatter_dimension=1, tiled=True)
        updated = (current.astype(jnp.float32) + gate_here * branch).astype(jnp.bfloat16)
        carried = from_behind(updated, "section", 1)
        finished = jnp.where((picked & is_valid)[:, None, None], updated[None], finished)
    returned = from_behind(finished, "section", -1)
    last_rows = jnp.where(section_id == 1, finished, returned).reshape(row_count, local_width)
    last_rows = lax.all_gather(last_rows, "tp", axis=1, tiled=True)
    final = modulate(last_rows, final_mod[0], final_mod[1])
    velocity = jnp.dot(final, w_final, preferred_element_type=jnp.float32)
    latent_next = latent + step_size[0] * velocity
    kv_next = lax.dynamic_index_in_dim(buffer, seq_id, 0, keepdims=False).reshape(
        1, 2, row_count, local_width
    )
    return (latent_next, kv_next)


def solution(mesh):
    return jax.shard_map(
        body,
        mesh=mesh,
        in_specs=(
            P(("req", "seq"), "tp"),
            P(("req", "seq"), ("section", "tp")),
            P("section", "seq", None, "tp"),
            P("section", "tp", None),
            P("section", None, None),
            P(),
            P(None, ("section", "tp")),
            P("section", None, ("req", "seq"), "tp"),
            P("section", None, "req", "tp"),
            P("req"),
            P("req", None),
            P(),
        ),
        out_specs=(P(("req", "seq"), ("section", "tp")), P("section", None, ("req", "seq"), "tp")),
        check_vma=False,
    )
```

profile of v0, /device:TPU:8, one launch (start us, length us, event | category | flops | bytes accessed | tf_op | source)
XLA Modules:
  0.0 890.9 jit_solution(9722535990750475162)
XLA Ops:
  16.4 12.3 %all-gather = bf16[1,32,1536]{2,1,0:T(8,128)(2,1)S(1)} all-gather(bf16[1,32,384]{2,1,0:T(8,128)(2,1)S(1)} %dynamic-slice_select_fusion), channel_id=2, replica_groups=mesh['req'=8,'section'=2,'seq'=8,'tp'=4] {'tp'}, dimensions={2}, use_global_device_ids=true | all-gather | bytes 122880 | tf_op jit(solution)/shard_map/all_gather | solution.py:109
  30.3 143.6 %all-gather.12.cloned.1.call-done = bf16[1,1536,3,384]{3,1,2,0:T(8,128)(2,1)} async-done(((bf16[1,192,3,384]{3,1,2,0:T(8,128)(2,1)}), bf16[1,1536,3,384]{3,1,2,0:T(8,128)(2,1)}) %all-gather.12.cloned.1.call-update) | async-done | bytes 3538960 | tf_op jit(solution)/shard_map/all_gather | solution.py:85
  173.9 6.1 copy.101
  183.2 54.6 %all-gather.2 = bf16[16,32,384]{2,1,0:T(8,128)(2,1)S(1)} all-gather(bf16[2,32,384]{2,1,0:T(8,128)(2,1)S(1)} %pad_maximum_fusion), channel_id=4, replica_groups=mesh['req'=8,'section'=2,'seq'=8,'tp'=4] {'seq'}, dimensions={0}, use_global_device_ids=true | all-gather | bytes 442368 | tf_op jit(solution)/shard_map/all_gather | solution.py:54
  237.8 38.7 %all-gather.10.cloned.1.call-done = bf16[8,2,128,384]{3,2,1,0:T(8,128)(2,1)} async-done(((bf16[1,2,128,384]{3,2,1,0:T(8,128)(2,1)}), bf16[8,2,128,384]{3,2,1,0:T(8,128)(2,1)}) %all-gather.10.cloned.1.call-update) | async-done | bytes 1572880 | tf_op jit(solution)/shard_map/all_gather | solution.py:94
  294.6 21.9 %reduce-scatter.6.cloned.1.call-done = f32[32,384]{1,0:T(8,128)} async-done(((f32[32,1536]{1,0:T(8,128)}), f32[32,384]{1,0:T(8,128)}) %reduce-scatter.6.cloned.1.call-update) | async-done | bytes 49168 | tf_op jit(solution)/shard_map/reduce_scatter | solution.py:123
  321.2 12.0 %all_gather.43 = bf16[32,1536]{1,0:T(8,128)(2,1)S(1)} all-gather(bf16[32,384]{1,0:T(8,128)(2,1)S(1)} %bitcast_select_fusion), channel_id=1, replica_groups=mesh['req'=8,'section'=2,'seq'=8,'tp'=4] {'tp'}, dimensions={1}, use_global_device_ids=true | all-gather | bytes 122880 | tf_op jit(solution)/shard_map/all_gather | solution.py:109
  337.5 65.7 %all-gather.3 = bf16[16,32,384]{2,1,0:T(8,128)(2,1)S(1)} all-gather(bf16[2,32,384]{2,1,0:T(8,128)(2,1)S(1)} %pad_maximum_fusion.1), channel_id=5, replica_groups=mesh['req'=8,'section'=2,'seq'=8,'tp'=4] {'seq'}, dimensions={0}, use_global_device_ids=true | all-gather | bytes 442368 | tf_op jit(solution)/shard_map/all_gather | solution.py:54
  405.3 3.7 reshape_squeeze.41
  416.1 3.7 reshape_squeeze.40
  427.5 25.8 %reduce-scatter.8.cloned.1.call-done = f32[32,384]{1,0:T(8,128)} async-done(((f32[32,1536]{1,0:T(8,128)}), f32[32,384]{1,0:T(8,128)}) %reduce-scatter.8.cloned.1.call-update) | async-done | bytes 49168 | tf_op jit(solution)/shard_map/reduce_scatter | solution.py:123
  460.7 12.0 %all_gather.45 = bf16[32,1536]{1,0:T(8,128)(2,1)S(1)} all-gather(bf16[32,384]{1,0:T(8,128)(2,1)S(1)} %bitcast_select_fusion.1), channel_id=1, replica_groups=mesh['req'=8,'section'=2,'seq'=8,'tp'=4] {'tp'}, dimensions={1}, use_global_device_ids=true | all-gather | bytes 122880 | tf_op jit(solution)/shard_map/all_gather | solution.py:109
  476.9 65.4 %all-gather.4 = bf16[16,32,384]{2,1,0:T(8,128)(2,1)S(1)} all-gather(bf16[2,32,384]{2,1,0:T(8,128)(2,1)S(1)} %pad_maximum_fusion.2), channel_id=6, replica_groups=mesh['req'=8,'section'=2,'seq'=8,'tp'=4] {'seq'}, dimensions={0}, use_global_device_ids=true | all-gather | bytes 442368 | tf_op jit(solution)/shard_map/all_gather | solution.py:54
  545.0 3.7 reshape_squeeze.43
  555.8 3.7 reshape_squeeze.42
  567.2 25.8 %reduce-scatter.10.cloned.1.call-done = f32[32,384]{1,0:T(8,128)} async-done(((f32[32,1536]{1,0:T(8,128)}), f32[32,384]{1,0:T(8,128)}) %reduce-scatter.10.cloned.1.call-update) | async-done | bytes 49168 | tf_op jit(solution)/shard_map/reduce_scatter | solution.py:123
  600.2 12.2 %all_gather.47 = bf16[32,1536]{1,0:T(8,128)(2,1)S(1)} all-gather(bf16[32,384]{1,0:T(8,128)(2,1)S(1)} %bitcast_select_fusion.2), channel_id=1, replica_groups=mesh['req'=8,'section'=2,'seq'=8,'tp'=4] {'tp'}, dimensions={1}, use_global_device_ids=true | all-gather | bytes 122880 | tf_op jit(solution)/shard_map/all_gather | solution.py:109
  616.6 65.3 %all-gather.5 = bf16[16,32,384]{2,1,0:T(8,128)(2,1)S(1)} all-gather(bf16[2,32,384]{2,1,0:T(8,128)(2,1)S(1)} %pad_maximum_fusion.3), channel_id=7, replica_groups=mesh['req'=8,'section'=2,'seq'=8,'tp'=4] {'seq'}, dimensions={0}, use_global_device_ids=true | all-gather | bytes 442368 | tf_op jit(solution)/shard_map/all_gather | solution.py:54
  696.0 3.7 reshape_squeeze.44
  709.9 23.3 %reduce-scatter.12.cloned.1.call-done = f32[32,384]{1,0:T(8,128)} async-done(((f32[32,1536]{1,0:T(8,128)}), f32[32,384]{1,0:T(8,128)}) %reduce-scatter.12.cloned.1.call-update) | async-done | bytes 49168 | tf_op jit(solution)/shard_map/reduce_scatter | solution.py:123
  740.3 12.0 %all_gather.49 = bf16[32,1536]{1,0:T(8,128)(2,1)S(1)} all-gather(bf16[32,384]{1,0:T(8,128)(2,1)S(1)} %bitcast_select_fusion.3), channel_id=1, replica_groups=mesh['req'=8,'section'=2,'seq'=8,'tp'=4] {'tp'}, dimensions={1}, use_global_device_ids=true | all-gather | bytes 122880 | tf_op jit(solution)/shard_map/all_gather | solution.py:109
  756.6 65.5 %all-gather.6 = bf16[16,32,384]{2,1,0:T(8,128)(2,1)S(1)} all-gather(bf16[2,32,384]{2,1,0:T(8,128)(2,1)S(1)} %pad_maximum_fusion.4), channel_id=8, replica_groups=mesh['req'=8,'section'=2,'seq'=8,'tp'=4] {'seq'}, dimensions={0}, use_global_device_ids=true | all-gather | bytes 442368 | tf_op jit(solution)/shard_map/all_gather | solution.py:54
  839.1 24.4 %reduce-scatter.14.cloned.1.call-done = f32[32,384]{1,0:T(8,128)} async-done(((f32[32,1536]{1,0:T(8,128)}), f32[32,384]{1,0:T(8,128)}) %reduce-scatter.14.cloned.1.call-update) | async-done | bytes 49168 | tf_op jit(solution)/shard_map/reduce_scatter | solution.py:123
  869.3 13.4 %all_gather.51 = bf16[128,1536]{1,0:T(8,128)(2,1)S(1)} all-gather(bf16[128,384]{1,0:T(8,128)(2,1)S(1)} %bitcast.206), channel_id=1, replica_groups=mesh['req'=8,'section'=2,'seq'=8,'tp'=4] {'tp'}, dimensions={1}, use_global_device_ids=true | all-gather | bytes 491520 | tf_op jit(solution)/shard_map/all_gather | solution.py:129
  (298 shorter events, 146.5 us)
Async XLA Ops:
  7.2 285.0 %copy-start = (bf16[1,384,1536]{2,1,0:T(8,128)(2,1)S(1)}, bf16[1,384,1536]{2,1,0:T(8,128)(2,1)}, u32[]{:S(2)}) copy-start(bf16[1,384,1536]{2,1,0:T(8,128)(2,1)} %param.15) | copy-start | bytes 3538948
  7.2 166.7 %all-gather.12.cloned.1.call-start = ((), (), s32[]{:S(2)}) async-start(), calls=%async_computation.11 | async-start | bytes 3981312 | tf_op jit(solution)/shard_map/all_gather | solution.py:85
  7.9 268.6 %all-gather.10.cloned.1.call-start = ((), (), s32[]{:S(2)}) async-start(), calls=%async_computation.5 | async-start | bytes 1769472 | tf_op jit(solution)/shard_map/all_gather | solution.py:94
  8.7 307.8 %reduce-scatter.6.cloned.1.call-start = ((), (), s32[]{:S(2)}) async-start(), calls=%async_computation.6 | async-start | bytes 245760 | tf_op jit(solution)/shard_map/reduce_scatter | solution.py:123
  13.5 269.7 %copy-start.3 = (bf16[1,1,154,384]{2,3,1,0:T(8,128)(2,1)}, bf16[1,1,154,384]{2,3,1,0:T(8,128)(2,1)S(1)}, u32[]{:S(2)}) copy-start(bf16[1,1,154,384]{2,3,1,0:T(8,128)(2,1)S(1)} %copy.106) | copy-start | bytes 354820
  29.6 246.9 %copy-start.34 = (pred[8,4]{1,0:T(8,128)(4,1)}, pred[8,4]{1,0:T(8,128)(4,1)S(1)}, u32[]{:S(2)}) copy-start(pred[8,4]{1,0:T(8,128)(4,1)S(1)} %fusion.204) | copy-start | bytes 100
  293.2 160.1 %reduce-scatter.8.cloned.1.call-start = ((), (), s32[]{:S(2)}) async-start(), calls=%async_computation.7 | async-start | bytes 245760 | tf_op jit(solution)/shard_map/reduce_scatter | solution.py:123
  317.3 3.9 collective-permute-start
  333.5 69.6 %copy-start.1 = (bf16[8,2,128,384]{3,2,1,0:T(8,128)(2,1)S(1)}, bf16[8,2,128,384]{3,2,1,0:T(8,128)(2,1)}, u32[]{:S(2)}) copy-start(bf16[8,2,128,384]{3,2,1,0:T(8,128)(2,1)} %all-gather.10.cloned.1.call-done) | copy-start | bytes 4718596
  333.5 69.6 %copy-start.35 = (pred[8,4]{1,0:T(8,128)(4,1)S(1)}, pred[8,4]{1,0:T(8,128)(4,1)}, u32[]{:S(2)}) copy-start(pred[8,4]{1,0:T(8,128)(4,1)} %copy-done.34) | copy-start | bytes 100
  333.6 69.6 %copy-start.39 = (pred[8,4]{1,0:T(8,128)(4,1)S(1)}, pred[8,4]{1,0:T(8,128)(4,1)}, u32[]{:S(2)}) copy-start(pred[8,4]{1,0:T(8,128)(4,1)} %fusion.205) | copy-start | bytes 100
  426.2 166.7 %reduce-scatter.10.cloned.1.call-start = ((), (), s32[]{:S(2)}) async-start(), calls=%async_computation.8 | async-start | bytes 245760 | tf_op jit(solution)/shard_map/reduce_scatter | solution.py:123
  454.7 5.3 collective-permute-start.1
  565.9 167.3 %reduce-scatter.12.cloned.1.call-start = ((), (), s32[]{:S(2)}) async-start(), calls=%async_computation.9 | async-start | bytes 245760 | tf_op jit(solution)/shard_map/reduce_scatter | solution.py:123
  594.4 5.1 collective-permute-start.2
  706.1 157.4 %reduce-scatter.14.cloned.1.call-start = ((), (), s32[]{:S(2)}) async-start(), calls=%async_computation.10 | async-start | bytes 245760 | tf_op jit(solution)/shard_map/reduce_scatter | solution.py:123
  734.6 4.9 collective-permute-start.3
  752.7 69.4 %copy-start.7 = (bf16[16,32,384]{2,1,0:T(8,128)(2,1)S(1)}, bf16[16,32,384]{2,1,0:T(8,128)(2,1)}, u32[]{:S(2)}) copy-start(bf16[16,32,384]{2,1,0:T(8,128)(2,1)} %copy-done.5) | copy-start | bytes 1179652
  752.7 69.4 %copy-start.9 = (bf16[16,32,384]{2,1,0:T(8,128)(2,1)S(1)}, bf16[16,32,384]{2,1,0:T(8,128)(2,1)}, u32[]{:S(2)}) copy-start(bf16[16,32,384]{2,1,0:T(8,128)(2,1)} %copy-done.8) | copy-start | bytes 1179652
  752.7 69.4 %copy-start.38 = (pred[8,4]{1,0:T(8,128)(4,1)S(1)}, pred[8,4]{1,0:T(8,128)(4,1)}, u32[]{:S(2)}) copy-start(pred[8,4]{1,0:T(8,128)(4,1)} %copy-done.34) | copy-start | bytes 100
  752.7 69.4 %copy-start.42 = (pred[8,4]{1,0:T(8,128)(4,1)S(1)}, pred[8,4]{1,0:T(8,128)(4,1)}, u32[]{:S(2)}) copy-start(pred[8,4]{1,0:T(8,128)(4,1)} %fusion.205) | copy-start | bytes 100
  752.7 69.4 %copy-start.46 = (pred[8,4]{1,0:T(8,128)(4,1)S(1)}, pred[8,4]{1,0:T(8,128)(4,1)}, u32[]{:S(2)}) copy-start(pred[8,4]{1,0:T(8,128)(4,1)} %fusion.206) | copy-start | bytes 100
  752.7 69.4 %copy-start.50 = (pred[8,4]{1,0:T(8,128)(4,1)S(1)}, pred[8,4]{1,0:T(8,128)(4,1)}, u32[]{:S(2)}) copy-start(pred[8,4]{1,0:T(8,128)(4,1)} %fusion.207) | copy-start | bytes 100
  865.3 3.2 collective-permute-start.4
  (48 other events, 1047.5 us)
Sparse Core Ops, SparseCore 0:
  11.2 162.6 all-gather.11
  177.1 99.3 all-gather.9
  293.3 23.0 reduce-scatter.5
  426.4 26.8 reduce-scatter.7
  566.0 26.8 reduce-scatter.9
  706.2 26.9 reduce-scatter.11
  836.6 26.8 reduce-scatter.13
where the time goes:
time: 894 us; the launch traced here: 891 us
  blocking collectives  390 us (44%)
  waiting for transfers between devices  305 us (34%)
  local copies, waits for them, and re-layouts  63.6 us (7%)
  matrix products  56.2 us (6%)
  other arithmetic  41.2 us (5%)
  between operations  26 us (3%)
    all_gather x5, blocking collectives, take_fresh(): arrived = lax.all_gather(new_kv_rows[None], 'seq', axis=0, tiled=True)  316 us
    all_gather x1, waiting for transfers between devices, body(): lax.all_gather(w_qkv[0], 'seq', axis=0, tiled=True)  144 us
    reduce_scatter x5, waiting for transfers between devices, body(): lax.psum_scatter(partial_value, 'tp', scatter_dimension=1, tiled=True)  121 us
    all_gather x5, blocking collectives, body(): full_rows = lax.all_gather(current, 'tp', axis=1, tiled=True)  60.4 us
    all_gather x1, waiting for transfers between devices, body(): lax.all_gather(stale_kv, 'seq', axis=0, tiled=True)  38.7 us
  transfers between devices with their start and end apart: 12, of which 8 were waited for; matrix products, arithmetic and copies ran while one was open for 4% of the time, Pallas kernels for 0%

commit v1 on v0

--- a/solution.py
+++ b/solution.py
@@ -51,7 +51,9 @@
 
 
 def take_fresh(new_kv_rows, column, is_valid, buffer, micro_ids):
-    arrived = lax.all_gather(new_kv_rows[None], "seq", axis=0, tiled=True)
+    arrived = jnp.concatenate(
+        lax.all_to_all(jnp.stack([new_kv_rows[None]] * lax.axis_size("seq")), "seq", 0, 0), axis=0
+    )
     hit_mask = (column[:, None] == micro_ids[None, :]) & is_valid
     return jnp.where(hit_mask[:, None, :, None, None], arrived[:, :, None], buffer)
 

time: 894 us -> 757 us (0.85)
  blocking collectives: 390 us -> 73.8 us
  waiting for transfers between devices: 305 us -> 403 us
  starting transfers between devices: 8.51 us -> 74 us
    all_gather x5 -> x0, blocking collectives: 316 us -> none  [take_fresh(): arrived = lax.all_gather(new_kv_rows[None], 'seq', axis=0, tiled=True)]
    all_to_all x0 -> x5, starting transfers between devices: none -> 65.7 us  [take_fresh(): lax.all_to_all(jnp.stack([new_kv_rows[None]] * lax.axis_size('seq')), 'se...]
    all_gather x1, waiting for transfers between devices: 38.7 us -> 96.5 us  [body(): lax.all_gather(stale_kv, 'seq', axis=0, tiled=True)]
    all_to_all x0 -> x5, waiting for transfers between devices: none -> 44.9 us  [take_fresh(): lax.all_to_all(jnp.stack([new_kv_rows[None]] * lax.axis_size('seq')), 'se...]
  transfers between devices with their start and end apart: 12 -> 17, of which waited for: 8 -> 12; matrix products, arithmetic and copies ran while one was open for 4% -> 6% of each run, Pallas kernels for 0% -> 0%
where the time goes in v1:
time: 757 us; the launch traced here: 753 us
  waiting for transfers between devices  403 us (53%)
  starting transfers between devices  74 us (10%)
  blocking collectives  73.8 us (10%)
  local copies, waits for them, and re-layouts  70 us (9%)
  matrix products  60.3 us (8%)
  other arithmetic  46.6 us (6%)
  between operations  25.7 us (3%)
    all_gather x1, waiting for transfers between devices, body(): lax.all_gather(w_qkv[0], 'seq', axis=0, tiled=True)  147 us
    reduce_scatter x5, waiting for transfers between devices, body(): lax.psum_scatter(partial_value, 'tp', scatter_dimension=1, tiled=True)  113 us
    all_gather x1, waiting for transfers between devices, body(): lax.all_gather(stale_kv, 'seq', axis=0, tiled=True)  96.5 us
    all_to_all x5, starting transfers between devices, take_fresh(): lax.all_to_all(jnp.stack([new_kv_rows[None]] * lax.axis_size('seq')), 'se...  65.7 us
    all_gather x5, blocking collectives, body(): full_rows = lax.all_gather(current, 'tp', axis=1, tiled=True)  60.4 us
    all_to_all x5, waiting for transfers between devices, take_fresh(): lax.all_to_all(jnp.stack([new_kv_rows[None]] * lax.axis_size('seq')), 'se...  44.9 us
    another operation x5, local copies, waits for them, and re-layouts, body(): all_keys = buffer[:, 0].reshape(-1, heads_here, HEAD)  17 us
    dot_general x5, matrix products, body(): jnp.dot(normed, projection, preferred_element_type=jnp.float32)  15.6 us
  transfers between devices with their start and end apart: 17, of which 12 were waited for; matrix products, arithmetic and copies ran while one was open for 6% of the time, Pallas kernels for 0%

profile of v1, /device:TPU:8, one launch (start us, length us, event | category | flops | bytes accessed | tf_op | source)
XLA Modules:
  0.0 753.4 jit_solution(7417442018095485374)
XLA Ops:
  13.2 12.3 %all-gather = bf16[1,32,1536]{2,1,0:T(8,128)(2,1)S(1)} all-gather(bf16[1,32,384]{2,1,0:T(8,128)(2,1)S(1)} %dynamic-slice_select_fusion), channel_id=2, replica_groups=mesh['req'=8,'section'=2,'seq'=8,'tp'=4] {'tp'}, dimensions={2}, use_global_device_ids=true | all-gather | bytes 122880 | tf_op jit(solution)/shard_map/all_gather | solution.py:111
  27.2 146.7 %all-gather.7.cloned.1.call-done = bf16[1,1536,3,384]{3,1,2,0:T(8,128)(2,1)} async-done(((bf16[1,192,3,384]{3,1,2,0:T(8,128)(2,1)}), bf16[1,1536,3,384]{3,1,2,0:T(8,128)(2,1)}) %all-gather.7.cloned.1.call-update) | async-done | bytes 3538960 | tf_op jit(solution)/shard_map/all_gather | solution.py:87
  173.9 6.1 copy.96
  183.9 5.1 all-to-all-start
  191.6 96.5 %all-gather.5.cloned.1.call-done = bf16[8,2,128,384]{3,2,1,0:T(8,128)(2,1)} async-done(((bf16[1,2,128,384]{3,2,1,0:T(8,128)(2,1)}), bf16[8,2,128,384]{3,2,1,0:T(8,128)(2,1)}) %all-gather.5.cloned.1.call-update) | async-done | bytes 1572880 | tf_op jit(solution)/shard_map/all_gather | solution.py:96
  306.7 19.2 %reduce-scatter.6.cloned.1.call-done = f32[32,384]{1,0:T(8,128)} async-done(((f32[32,1536]{1,0:T(8,128)}), f32[32,384]{1,0:T(8,128)}) %reduce-scatter.6.cloned.1.call-update) | async-done | bytes 49168 | tf_op jit(solution)/shard_map/reduce_scatter | solution.py:125
  330.8 12.0 %all_gather.27 = bf16[32,1536]{1,0:T(8,128)(2,1)S(1)} all-gather(bf16[32,384]{1,0:T(8,128)(2,1)S(1)} %bitcast_select_fusion), channel_id=1, replica_groups=mesh['req'=8,'section'=2,'seq'=8,'tp'=4] {'tp'}, dimensions={1}, use_global_device_ids=true | all-gather | bytes 122880 | tf_op jit(solution)/shard_map/all_gather | solution.py:111
  347.7 15.2 %all-to-all-start.1 = ((bf16[8,1,2,32,384]{4,3,2,1,0:T(8,128)(2,1)}), bf16[8,1,2,32,384]{4,3,2,1,0:T(8,128)(2,1)S(1)}, u32[]{:S(2)}, u32[]{:S(2)}) async-start(bf16[8,1,2,32,384]{4,3,2,1,0:T(8,128)(2,1)} %stack.67), calls=%async_computation.2 | async-start | bytes 786432 | tf_op jit(solution)/shard_map/all_to_all | solution.py:55
  368.1 11.8 %all-to-all-done.1 = bf16[8,1,2,32,384]{4,3,2,1,0:T(8,128)(2,1)S(1)} async-done(((bf16[8,1,2,32,384]{4,3,2,1,0:T(8,128)(2,1)}), bf16[8,1,2,32,384]{4,3,2,1,0:T(8,128)(2,1)S(1)}, u32[]{:S(2)}, u32[]{:S(2)}) %all-to-all-start.1) | async-done | bytes 393248 | tf_op jit(solution)/shard_map/all_to_all | solution.py:55
  391.0 3.7 reshape_squeeze.40
  401.1 24.0 %reduce-scatter.8.cloned.1.call-done = f32[32,384]{1,0:T(8,128)} async-done(((f32[32,1536]{1,0:T(8,128)}), f32[32,384]{1,0:T(8,128)}) %reduce-scatter.8.cloned.1.call-update) | async-done | bytes 49168 | tf_op jit(solution)/shard_map/reduce_scatter | solution.py:125
  432.1 12.0 %all_gather.28 = bf16[32,1536]{1,0:T(8,128)(2,1)S(1)} all-gather(bf16[32,384]{1,0:T(8,128)(2,1)S(1)} %bitcast_select_fusion.1), channel_id=1, replica_groups=mesh['req'=8,'section'=2,'seq'=8,'tp'=4] {'tp'}, dimensions={1}, use_global_device_ids=true | all-gather | bytes 122880 | tf_op jit(solution)/shard_map/all_gather | solution.py:111
  449.0 15.1 %all-to-all-start.2 = ((bf16[8,1,2,32,384]{4,3,2,1,0:T(8,128)(2,1)}), bf16[8,1,2,32,384]{4,3,2,1,0:T(8,128)(2,1)}, u32[]{:S(2)}, u32[]{:S(2)}) async-start(bf16[8,1,2,32,384]{4,3,2,1,0:T(8,128)(2,1)} %stack.71), calls=%async_computation.4 | async-start | bytes 786432 | tf_op jit(solution)/shard_map/all_to_all | solution.py:55
  469.3 11.9 %all-to-all-done.2 = bf16[8,1,2,32,384]{4,3,2,1,0:T(8,128)(2,1)} async-done(((bf16[8,1,2,32,384]{4,3,2,1,0:T(8,128)(2,1)}), bf16[8,1,2,32,384]{4,3,2,1,0:T(8,128)(2,1)}, u32[]{:S(2)}, u32[]{:S(2)}) %all-to-all-start.2) | async-done | bytes 393248 | tf_op jit(solution)/shard_map/all_to_all | solution.py:55
  503.3 24.1 %reduce-scatter.10.cloned.1.call-done = f32[32,384]{1,0:T(8,128)} async-done(((f32[32,1536]{1,0:T(8,128)}), f32[32,384]{1,0:T(8,128)}) %reduce-scatter.10.cloned.1.call-update) | async-done | bytes 49168 | tf_op jit(solution)/shard_map/reduce_scatter | solution.py:125
  534.7 12.2 %all_gather.29 = bf16[32,1536]{1,0:T(8,128)(2,1)S(1)} all-gather(bf16[32,384]{1,0:T(8,128)(2,1)S(1)} %bitcast_select_fusion.2), channel_id=1, replica_groups=mesh['req'=8,'section'=2,'seq'=8,'tp'=4] {'tp'}, dimensions={1}, use_global_device_ids=true | all-gather | bytes 122880 | tf_op jit(solution)/shard_map/all_gather | solution.py:111
  551.8 15.1 %all-to-all-start.3 = ((bf16[8,1,2,32,384]{4,3,2,1,0:T(8,128)(2,1)}), bf16[8,1,2,32,384]{4,3,2,1,0:T(8,128)(2,1)}, u32[]{:S(2)}, u32[]{:S(2)}) async-start(bf16[8,1,2,32,384]{4,3,2,1,0:T(8,128)(2,1)} %stack.75), calls=%async_computation.6 | async-start | bytes 786432 | tf_op jit(solution)/shard_map/all_to_all | solution.py:55
  572.0 11.6 %all-to-all-done.3 = bf16[8,1,2,32,384]{4,3,2,1,0:T(8,128)(2,1)} async-done(((bf16[8,1,2,32,384]{4,3,2,1,0:T(8,128)(2,1)}), bf16[8,1,2,32,384]{4,3,2,1,0:T(8,128)(2,1)}, u32[]{:S(2)}, u32[]{:S(2)}) %all-to-all-start.3) | async-done | bytes 393248 | tf_op jit(solution)/shard_map/all_to_all | solution.py:55
  606.3 24.1 %reduce-scatter.12.cloned.1.call-done = f32[32,384]{1,0:T(8,128)} async-done(((f32[32,1536]{1,0:T(8,128)}), f32[32,384]{1,0:T(8,128)}) %reduce-scatter.12.cloned.1.call-update) | async-done | bytes 49168 | tf_op jit(solution)/shard_map/reduce_scatter | solution.py:125
  637.7 12.0 %all_gather.30 = bf16[32,1536]{1,0:T(8,128)(2,1)S(1)} all-gather(bf16[32,384]{1,0:T(8,128)(2,1)S(1)} %bitcast_select_fusion.3), channel_id=1, replica_groups=mesh['req'=8,'section'=2,'seq'=8,'tp'=4] {'tp'}, dimensions={1}, use_global_device_ids=true | all-gather | bytes 122880 | tf_op jit(solution)/shard_map/all_gather | solution.py:111
  654.6 15.1 %all-to-all-start.4 = ((bf16[8,1,2,32,384]{4,3,2,1,0:T(8,128)(2,1)}), bf16[8,1,2,32,384]{4,3,2,1,0:T(8,128)(2,1)}, u32[]{:S(2)}, u32[]{:S(2)}) async-start(bf16[8,1,2,32,384]{4,3,2,1,0:T(8,128)(2,1)} %stack.79), calls=%async_computation.8 | async-start | bytes 786432 | tf_op jit(solution)/shard_map/all_to_all | solution.py:55
  676.6 9.6 %all-to-all-done.4 = bf16[8,1,2,32,384]{4,3,2,1,0:T(8,128)(2,1)} async-done(((bf16[8,1,2,32,384]{4,3,2,1,0:T(8,128)(2,1)}), bf16[8,1,2,32,384]{4,3,2,1,0:T(8,128)(2,1)}, u32[]{:S(2)}, u32[]{:S(2)}) %all-to-all-start.4) | async-done | bytes 393248 | tf_op jit(solution)/shard_map/all_to_all | solution.py:55
  704.1 21.9 %reduce-scatter.14.cloned.1.call-done = f32[32,384]{1,0:T(8,128)} async-done(((f32[32,1536]{1,0:T(8,128)}), f32[32,384]{1,0:T(8,128)}) %reduce-scatter.14.cloned.1.call-update) | async-done | bytes 49168 | tf_op jit(solution)/shard_map/reduce_scatter | solution.py:125
  731.8 13.3 %all_gather.31 = bf16[128,1536]{1,0:T(8,128)(2,1)S(1)} all-gather(bf16[128,384]{1,0:T(8,128)(2,1)S(1)} %bitcast.236), channel_id=1, replica_groups=mesh['req'=8,'section'=2,'seq'=8,'tp'=4] {'tp'}, dimensions={1}, use_global_device_ids=true | all-gather | bytes 491520 | tf_op jit(solution)/shard_map/all_gather | solution.py:131
  (286 shorter events, 177.1 us)
Async XLA Ops:
  7.2 297.8 %copy-start = (bf16[1,384,1536]{2,1,0:T(8,128)(2,1)S(1)}, bf16[1,384,1536]{2,1,0:T(8,128)(2,1)}, u32[]{:S(2)}) copy-start(bf16[1,384,1536]{2,1,0:T(8,128)(2,1)} %param.15) | copy-start | bytes 3538948
  7.2 166.7 %all-gather.7.cloned.1.call-start = ((), (), s32[]{:S(2)}) async-start(), calls=%async_computation.16 | async-start | bytes 3981312 | tf_op jit(solution)/shard_map/all_gather | solution.py:87
  7.9 280.1 %all-gather.5.cloned.1.call-start = ((), (), s32[]{:S(2)}) async-start(), calls=%async_computation.10 | async-start | bytes 1769472 | tf_op jit(solution)/shard_map/all_gather | solution.py:96
  183.9 104.1 %all-to-all-start = ((bf16[8,1,2,32,384]{4,3,2,1,0:T(8,128)(2,1)}), bf16[8,1,2,32,384]{4,3,2,1,0:T(8,128)(2,1)S(1)}, u32[]{:S(2)}, u32[]{:S(2)}) async-start(bf16[8,1,2,32,384]{4,3,2,1,0:T(8,128)(2,1)} %stack.63), calls=%async_computation | async-start | bytes 786432 | tf_op jit(solution)/shard_map/all_to_all | solution.py:55
  189.0 136.8 %reduce-scatter.6.cloned.1.call-start = ((), (), s32[]{:S(2)}) async-start(), calls=%async_computation.11 | async-start | bytes 245760 | tf_op jit(solution)/shard_map/reduce_scatter | solution.py:125
  189.6 100.4 %copy-start.3 = (bf16[1,1,154,384]{2,3,1,0:T(8,128)(2,1)}, bf16[1,1,154,384]{2,3,1,0:T(8,128)(2,1)S(1)}, u32[]{:S(2)}) copy-start(bf16[1,1,154,384]{2,3,1,0:T(8,128)(2,1)S(1)} %copy.101) | copy-start | bytes 354820
  191.1 98.8 %copy-start.39 = (pred[154]{0:T(512)(128)(4,1)}, pred[154]{0:T(512)(128)(4,1)S(1)}, u32[]{:S(2)}) copy-start(pred[154]{0:T(512)(128)(4,1)S(1)} %iota_compare_fusion.5) | copy-start | bytes 466
  191.2 98.7 %copy-start.32 = (pred[8,4]{1,0:T(8,128)(4,1)}, pred[8,4]{1,0:T(8,128)(4,1)S(1)}, u32[]{:S(2)}) copy-start(pred[8,4]{1,0:T(8,128)(4,1)S(1)} %fusion.204) | copy-start | bytes 100
  326.7 4.1 collective-permute-start
  346.3 33.6 %copy-start.1 = (bf16[8,2,128,384]{3,2,1,0:T(8,128)(2,1)S(1)}, bf16[8,2,128,384]{3,2,1,0:T(8,128)(2,1)}, u32[]{:S(2)}) copy-start(bf16[8,2,128,384]{3,2,1,0:T(8,128)(2,1)} %all-gather.5.cloned.1.call-done) | copy-start | bytes 4718596
  347.7 32.2 %all-to-all-start.1 = ((bf16[8,1,2,32,384]{4,3,2,1,0:T(8,128)(2,1)}), bf16[8,1,2,32,384]{4,3,2,1,0:T(8,128)(2,1)S(1)}, u32[]{:S(2)}, u32[]{:S(2)}) async-start(bf16[8,1,2,32,384]{4,3,2,1,0:T(8,128)(2,1)} %stack.67), calls=%async_computation.2 | async-start | bytes 786432 | tf_op jit(solution)/shard_map/all_to_all | solution.py:55
  362.9 62.2 %reduce-scatter.8.cloned.1.call-start = ((), (), s32[]{:S(2)}) async-start(), calls=%async_computation.12 | async-start | bytes 245760 | tf_op jit(solution)/shard_map/reduce_scatter | solution.py:125
  426.5 4.9 collective-permute-start.1
  449.0 32.1 %all-to-all-start.2 = ((bf16[8,1,2,32,384]{4,3,2,1,0:T(8,128)(2,1)}), bf16[8,1,2,32,384]{4,3,2,1,0:T(8,128)(2,1)}, u32[]{:S(2)}, u32[]{:S(2)}) async-start(bf16[8,1,2,32,384]{4,3,2,1,0:T(8,128)(2,1)} %stack.71), calls=%async_computation.4 | async-start | bytes 786432 | tf_op jit(solution)/shard_map/all_to_all | solution.py:55
  464.2 63.2 %reduce-scatter.10.cloned.1.call-start = ((), (), s32[]{:S(2)}) async-start(), calls=%async_computation.13 | async-start | bytes 245760 | tf_op jit(solution)/shard_map/reduce_scatter | solution.py:125
  528.8 5.1 collective-permute-start.2
  551.8 31.8 %all-to-all-start.3 = ((bf16[8,1,2,32,384]{4,3,2,1,0:T(8,128)(2,1)}), bf16[8,1,2,32,384]{4,3,2,1,0:T(8,128)(2,1)}, u32[]{:S(2)}, u32[]{:S(2)}) async-start(bf16[8,1,2,32,384]{4,3,2,1,0:T(8,128)(2,1)} %stack.75), calls=%async_computation.6 | async-start | bytes 786432 | tf_op jit(solution)/shard_map/all_to_all | solution.py:55
  566.9 63.5 %reduce-scatter.12.cloned.1.call-start = ((), (), s32[]{:S(2)}) async-start(), calls=%async_computation.14 | async-start | bytes 245760 | tf_op jit(solution)/shard_map/reduce_scatter | solution.py:125
  631.8 5.1 collective-permute-start.3
  654.6 31.6 %all-to-all-start.4 = ((bf16[8,1,2,32,384]{4,3,2,1,0:T(8,128)(2,1)}), bf16[8,1,2,32,384]{4,3,2,1,0:T(8,128)(2,1)}, u32[]{:S(2)}, u32[]{:S(2)}) async-start(bf16[8,1,2,32,384]{4,3,2,1,0:T(8,128)(2,1)} %stack.79), calls=%async_computation.8 | async-start | bytes 786432 | tf_op jit(solution)/shard_map/all_to_all | solution.py:55
  669.7 56.3 %reduce-scatter.14.cloned.1.call-start = ((), (), s32[]{:S(2)}) async-start(), calls=%async_computation.15 | async-start | bytes 245760 | tf_op jit(solution)/shard_map/reduce_scatter | solution.py:125
  701.6 44.0 %copy-start.47 = (bf16[1536,8]{0,1:T(8,128)(2,1)S(1)}, bf16[1536,8]{0,1:T(8,128)(2,1)}, u32[]{:S(2)}) copy-start(bf16[1536,8]{0,1:T(8,128)(2,1)} %param.18) | copy-start | bytes 73732
  701.6 44.0 %copy-start.48 = (f32[128,8]{0,1:T(8,128)S(1)}, f32[128,8]{0,1:T(8,128)}, u32[]{:S(2)}) copy-start(f32[128,8]{0,1:T(8,128)} %param.13) | copy-start | bytes 12292
  727.7 3.2 collective-permute-start.4
  (42 other events, 422.8 us)
Sparse Core Ops, SparseCore 0:
  11.1 162.7 all-gather.6
  177.1 110.9 all-gather.4
  306.1 19.7 reduce-scatter.5
  401.2 23.8 reduce-scatter.7
  503.4 23.9 reduce-scatter.9
  606.4 23.9 reduce-scatter.11
  701.7 24.2 reduce-scatter.13
